TPU v7x, 256 devices: a whole 4x4x8 slice. The times are simulated.
256 devices in a mesh: pb: 64 (over z, y_hi, x), br: 4 (over y_lo, core).
Axes of the slice: x: 4, y: 4 (y_hi: 2, y_lo: 2; y = y_hi * 2 + y_lo), z: 8, core: 2. Of those that a mesh axis runs over, the one named last changes fastest.
Arguments:
- bloch_const: bfloat16 [36, 663552], P(None, 'pb'), may hold values from -1 to 1
- polarization: bfloat16 [36, 512, 36], P('br', 'pb'), may hold values from -1 to 1
- delta_weight: bfloat16 [36, 512, 18432], P('br', None, 'pb'), may hold values from 0.02 to 3
- partner: int32 [512, 512], P('pb'), may hold values from 0 to 511, each once within a row
- velocity: float32 [512, 36], P('pb', 'br'), may hold values from -0.5 to 1.5
- capacity: float32 [512, 36], P('pb', 'br'), may hold values from 0.2 to 2
Outputs:
- deviation: float32 [512, 36], P('pb', 'br')
- kappa: float32 [2], replicated
Inputs may be any that keep to these rules, and one draw needn't show every extreme that they name: For each q, partner[q, :] names every q-point exactly once.
All inputs are finite; a program needn't handle non-finite values.
Results may differ from a plain program's by a relative error of at most 0.0003.
Values may be sent and summed in bfloat16 or wider, within the bound.
A program may use at most 192 MiB of HBM per device.

v0:
```python
from functools import partial
import jax
import jax.numpy as jnp
from jax import lax
from jax.sharding import PartitionSpec as P

ITERS = 2


def split_points(bloch_const, local_points, chosen):
    components = bloch_const.shape[0]
    reshaped = bloch_const.reshape(components, local_points, -1, components)
    return jnp.transpose(reshaped.reshape(components, local_points, chosen * components), (1, 0, 2))


def coupling_fold(carried, shard_in, first_row, const_blocks, delta_local, inv_count):
    lead_size = shard_in.shape[0]
    piece_len = shard_in.shape[1]
    components = shard_in.shape[2]
    flat_rows = shard_in.reshape(lead_size * piece_len, components)

    def per_point(const_block):
        amplitude = jnp.dot(flat_rows, const_block, preferred_element_type=jnp.float32)
        amplitude = amplitude.reshape(lead_size * piece_len, -1, components)
        return jnp.sum(amplitude * amplitude, axis=2)

    squared = lax.map(per_point, const_blocks)
    squared = jnp.transpose(squared, (1, 0, 2)).reshape(lead_size, piece_len, -1)
    weight_block = delta_local.astype(jnp.float32)
    return squared * weight_block * inv_count


def branch_total(partial_sum):
    own_count = partial_sum.shape[1] // lax.axis_size("br")
    summed = lax.psum(partial_sum, "br")
    return lax.dynamic_slice_in_dim(summed, lax.axis_index("br") * own_count, own_count, 1)


def full_deviation(deviation):
    return lax.all_gather(deviation, "pb", axis=0, tiled=True)


def on_device(bloch_const, polarization, delta_weight, partner, velocity, capacity):
    local_points = velocity.shape[0]
    own_count = velocity.shape[1]
    all_branches = own_count * lax.axis_size("br")
    total_points = polarization.shape[1] * lax.axis_size("pb")
    inv_count = 1.0 / (total_points * all_branches)
    const_blocks = split_points(bloch_const, local_points, all_branches)
    zero_start = jnp.zeros((own_count, total_points, local_points * all_branches), jnp.float32)
    folder = partial(
        coupling_fold, const_blocks=const_blocks, delta_local=delta_weight, inv_count=inv_count
    )
    coupling = folder(
        zero_start, lax.all_gather(polarization, "pb", axis=1, tiled=True), jnp.int32(0)
    )
    coupling = coupling.reshape(own_count, total_points, local_points, all_branches)
    rate_total = branch_total(jnp.sum(coupling, axis=(0, 1)))
    deviation = velocity / rate_total
    heat_weight = capacity * velocity
    kappas = []
    for sweep_index in range(ITERS):
        deviation_all = full_deviation(deviation)
        partner_value = deviation_all[partner]
        combined = jnp.transpose(deviation_all)[:, :, None] + jnp.transpose(
            partner_value, (2, 1, 0)
        )
        spread = jnp.einsum("abqs,abq->qs", coupling, combined, precision=lax.Precision.HIGHEST)
        spread = branch_total(spread)
        deviation = (velocity + 0.5 * spread) / rate_total
        kappa_term = jnp.sum(heat_weight * deviation) * inv_count
        kappas.append(lax.psum(kappa_term, ("pb", "br")))
    kappa = jnp.stack(kappas)
    return (deviation, kappa)


def solution(mesh):
    in_specs = (
        P(None, "pb"),
        P("br", "pb", None),
        P("br", None, "pb"),
        P("pb", None),
        P("pb", "br"),
        P("pb", "br"),
    )
    out_specs = (P("pb", "br"), P())
    return jax.shard_map(
        on_device, mesh=mesh, in_specs=in_specs, out_specs=out_specs, check_vma=False
    )
```

profile of v0, /device:TPU:1, one launch (start us, length us, event | category | flops | bytes accessed | tf_op | source)
XLA Modules:
  0.0 1065.5 jit_solution(7599198885120095185)
XLA Ops:
  0.6 2.4 reshape_reshape.3
  3.1 163.8 %all_gather.9 = bf16[9,512,36]{2,1,0:T(8,128)(2,1)S(1)} all-gather(bf16[9,8,36]{2,1,0:T(8,128)(2,1)} %param.9), channel_id=1, replica_groups=mesh['pb'=64,'br'=4] {'pb'}, dimensions={1}, use_global_device_ids=true | all-gather | bytes 336960 | tf_op jit(solution)/shard_map/all_gather | solution.py:55
  166.9 349.9 %while.10 = (s32[]{:T(128)}, f32[8,4608,36]{1,2,0:T(8,128)}, bf16[8,36,1296]{2,1,0:T(8,128)(2,1)S(1)}, bf16[4608,36]{1,0:T(8,128)(2,1)S(1)}, s32[]{:T(128)}, /*index=5*/f32[]{:T(128)}) while((s32[]{:T(128)}, f32[8,4608,36]{1,2,0:T(8,128)}, bf16[8,36,1296]{2,1,0:T(8,128)(2,1)S(1)}, bf16[4608,36]{1,0:T(8,128)(2,1)S(1)}, s32[]{:T(128)}, ...), condition=%wide.region_2.3_spmd, body=%wide.region_0.2_spmd.sunk | while | flops 441759744 | bytes 98908744 | solution.py:27
  166.9 9.7 fusion.18
  176.6 23.2 %mul.74 = f32[4608,36,36]{0,2,1:T(8,128)} reshape(f32[4608,1296]{0,1:T(8,128)} %fusion.18) | data formatting | bytes 47775744 | tf_op jit(solution)/shard_map/while/body/eval_jaxpr/mul | solution.py:25
  199.8 9.9 reduce_sum.46
  209.7 0.9 bitcast_dynamic-update-slice_fusion.2
  210.6 9.7 fusion.18
  220.3 23.2 %mul.74 = f32[4608,36,36]{0,2,1:T(8,128)} reshape(f32[4608,1296]{0,1:T(8,128)} %fusion.18) | data formatting | bytes 47775744 | tf_op jit(solution)/shard_map/while/body/eval_jaxpr/mul | solution.py:25
  243.5 9.9 reduce_sum.46
  253.5 0.9 bitcast_dynamic-update-slice_fusion.2
  254.4 9.7 fusion.18
  264.1 23.2 %mul.74 = f32[4608,36,36]{0,2,1:T(8,128)} reshape(f32[4608,1296]{0,1:T(8,128)} %fusion.18) | data formatting | bytes 47775744 | tf_op jit(solution)/shard_map/while/body/eval_jaxpr/mul | solution.py:25
  287.3 9.9 reduce_sum.46
  297.2 0.9 bitcast_dynamic-update-slice_fusion.2
  298.1 9.7 fusion.18
  307.9 23.2 %mul.74 = f32[4608,36,36]{0,2,1:T(8,128)} reshape(f32[4608,1296]{0,1:T(8,128)} %fusion.18) | data formatting | bytes 47775744 | tf_op jit(solution)/shard_map/while/body/eval_jaxpr/mul | solution.py:25
  331.0 9.9 reduce_sum.46
  341.9 9.7 fusion.18
  351.6 23.2 %mul.74 = f32[4608,36,36]{0,2,1:T(8,128)} reshape(f32[4608,1296]{0,1:T(8,128)} %fusion.18) | data formatting | bytes 47775744 | tf_op jit(solution)/shard_map/while/body/eval_jaxpr/mul | solution.py:25
  374.7 9.9 reduce_sum.46
  385.6 9.7 fusion.18
  395.3 23.2 %mul.74 = f32[4608,36,36]{0,2,1:T(8,128)} reshape(f32[4608,1296]{0,1:T(8,128)} %fusion.18) | data formatting | bytes 47775744 | tf_op jit(solution)/shard_map/while/body/eval_jaxpr/mul | solution.py:25
  418.5 9.9 reduce_sum.46
  428.4 0.9 bitcast_dynamic-update-slice_fusion.2
  429.4 9.7 fusion.18
  439.1 23.2 %mul.74 = f32[4608,36,36]{0,2,1:T(8,128)} reshape(f32[4608,1296]{0,1:T(8,128)} %fusion.18) | data formatting | bytes 47775744 | tf_op jit(solution)/shard_map/while/body/eval_jaxpr/mul | solution.py:25
  462.2 9.9 reduce_sum.46
  473.1 9.7 fusion.18
  482.8 23.2 %mul.74 = f32[4608,36,36]{0,2,1:T(8,128)} reshape(f32[4608,1296]{0,1:T(8,128)} %fusion.18) | data formatting | bytes 47775744 | tf_op jit(solution)/shard_map/while/body/eval_jaxpr/mul | solution.py:25
  506.0 9.9 reduce_sum.46
  515.9 0.9 bitcast_dynamic-update-slice_fusion.2
  516.8 7.2 reshape.19
  524.1 9.9 fusion.9
  534.0 33.8 %psum.35 = f32[8,36]{1,0:T(8,128)S(1)} all-reduce(f32[8,36]{1,0:T(8,128)S(1)} %reduce_sum.39), channel_id=1, replica_groups=mesh['pb'=64,'br'=4] {'br'}, use_global_device_ids=true, to_apply=%region_4.5 | all-reduce | flops 288 | bytes 2304 | tf_op jit(solution)/shard_map/psum | solution.py:35
  567.9 147.9 %all_gather.10 = f32[512,9]{1,0:T(8,128)S(1)} all-gather(f32[8,9]{1,0:T(8,128)S(1)} %dynamic-slice_divide_fusion), channel_id=1, replica_groups=mesh['pb'=64,'br'=4] {'pb'}, dimensions={0}, use_global_device_ids=true | all-gather | bytes 18720 | tf_op jit(solution)/shard_map/all_gather | solution.py:40
  715.9 14.1 %gather_fusion = f32[4096,9]{1,0:T(8,128)} fusion(f32[512,9]{1,0:T(8,128)S(1)} %all_gather.10, s32[4096]{0:T(1024)S(1)} %broadcast_clamp_fusion), kind=kCustom, calls=%fused_computation | custom fusion | bytes 311296 | tf_op jit(solution)/shard_map/gather | solution.py:64
  729.9 1.7 add_bitcast_fusion.1
  732.5 11.1 %fusion.6 = f32[8,1,36,1]{2,1,0,3:T(1,128)S(1)} fusion(f32[9,512,8,1]{1,3,2,0:T(1,128)S(1)} %copy.15, f32[9,512,8,36]{1,0,3,2:T(8,128)} %bitcast.51), kind=kOutput, calls=%fused_computation.11 | convolution fusion | flops 15925248 | bytes 5457024 | tf_op jit(solution)/shard_map/abqs,abq->qs/dot_general | solution.py:68
  743.6 33.2 %psum.36 = f32[8,36]{1,0:T(8,128)S(1)} all-reduce(f32[8,36]{1,0:T(8,128)S(1)} %bitcast.60), channel_id=1, replica_groups=mesh['pb'=64,'br'=4] {'br'}, use_global_device_ids=true, to_apply=%region_5.6 | all-reduce | flops 288 | bytes 2304 | tf_op jit(solution)/shard_map/psum | solution.py:35
  776.9 149.5 %all_gather.11 = f32[512,9]{1,0:T(8,128)S(1)} all-gather(f32[8,9]{1,0:T(8,128)S(1)} %add_divide_fusion.1), channel_id=1, replica_groups=mesh['pb'=64,'br'=4] {'pb'}, dimensions={0}, use_global_device_ids=true | all-gather | bytes 18720 | tf_op jit(solution)/shard_map/all_gather | solution.py:40
  926.4 14.1 %gather_fusion.1 = f32[4096,9]{1,0:T(8,128)} fusion(f32[512,9]{1,0:T(8,128)S(1)} %all_gather.11, s32[4096]{0:T(1024)S(1)} %broadcast_clamp_fusion), kind=kCustom, calls=%fused_computation.1 | custom fusion | bytes 311296 | tf_op jit(solution)/shard_map/gather | solution.py:64
  940.5 1.8 add_bitcast_fusion
  943.0 11.1 %fusion.4 = f32[8,1,36,1]{2,1,0,3:T(1,128)S(1)} fusion(f32[9,512,8,1]{1,3,2,0:T(1,128)S(1)} %copy.17, f32[9,512,8,36]{1,0,3,2:T(8,128)} %bitcast.52), kind=kOutput, calls=%fused_computation.9 | convolution fusion | flops 15925248 | bytes 5457024 | tf_op jit(solution)/shard_map/abqs,abq->qs/dot_general | solution.py:68
  954.2 33.4 %psum.37 = f32[8,36]{1,0:T(8,128)S(1)} all-reduce(f32[8,36]{1,0:T(8,128)S(1)} %bitcast.59), channel_id=1, replica_groups=mesh['pb'=64,'br'=4] {'br'}, use_global_device_ids=true, to_apply=%region_6.7 | all-reduce | flops 288 | bytes 2304 | tf_op jit(solution)/shard_map/psum | solution.py:35
  987.6 1.3 multiply_reduce_fusion.1
  990.1 73.6 %all-reduce = (f32[1]{0:T(128)}, f32[1]{0:T(128)}) all-reduce(f32[1]{0:T(128)} %bitcast.20, f32[1]{0:T(128)} %bitcast.19), channel_id=1, replica_groups=mesh['pb'=64,'br'=4] {'pb','br'}, use_global_device_ids=true, to_apply=%region_10.11 | all-reduce | flops 2 | bytes 16 | tf_op jit(solution)/shard_map/psum | solution.py:72
  1063.7 1.8 pad_maximum_fusion
  (21 shorter events, 4.8 us)
Async XLA Ops:
  516.8 7.2 copy-start
  524.1 43.8 %copy-start.1 = (f32[8,9]{1,0:T(8,128)S(1)}, f32[8,9]{1,0:T(8,128)}, u32[]{:S(2)}) copy-start(f32[8,9]{1,0:T(8,128)} %param.12) | copy-start | bytes 868
  524.1 191.8 %copy-start.2 = (s32[8,512]{1,0:T(8,128)S(1)}, s32[8,512]{1,0:T(8,128)}, u32[]{:S(2)}) copy-start(s32[8,512]{1,0:T(8,128)} %param.11) | copy-start | bytes 49156
  940.4 47.1 %copy-start.3 = (f32[8,9]{1,0:T(8,128)S(1)}, f32[8,9]{1,0:T(8,128)}, u32[]{:S(2)}) copy-start(f32[8,9]{1,0:T(8,128)} %param.13) | copy-start | bytes 868
where the time goes:
time: 1070 us
  blocking collectives  635 us (59%)
  local copies, waits for them, and re-layouts  232 us (22%)
  matrix products  99.9 us (9%)
  other arithmetic  96.2 us (9%)
    all_gather x2, blocking collectives, full_deviation(): return lax.all_gather(deviation, 'pb', axis=0, tiled=True)  297 us
    mul x8, local copies, waits for them, and re-layouts, per_point(): return jnp.sum(amplitude * amplitude, axis=2)  185 us
    all_gather x1, blocking collectives, on_device(): lax.all_gather(polarization, 'pb', axis=1, tiled=True)  164 us
    psum x3, blocking collectives, branch_total(): summed = lax.psum(partial_sum, 'br')  100 us
    reduce_sum x8, other arithmetic, per_point(): return jnp.sum(amplitude * amplitude, axis=2)  79.6 us
    dot_general x8, matrix products, per_point(): jnp.dot(flat_rows, const_block, preferred_element_type=jnp.float32)  77.6 us
    psum x1, blocking collectives, on_device(): kappas.append(lax.psum(kappa_term, ('pb', 'br')))  73.6 us
    gather x2, local copies, waits for them, and re-layouts, on_device(): partner_value = deviation_all[partner]  28.1 us

commit v1 on v0

--- a/solution.py
+++ b/solution.py
@@ -52,7 +52,11 @@
         coupling_fold, const_blocks=const_blocks, delta_local=delta_weight, inv_count=inv_count
     )
     coupling = folder(
-        zero_start, lax.all_gather(polarization, "pb", axis=1, tiled=True), jnp.int32(0)
+        zero_start,
+        jnp.concatenate(
+            lax.all_to_all(jnp.stack([polarization] * lax.axis_size("pb")), "pb", 0, 0), axis=1
+        ),
+        jnp.int32(0),
     )
     coupling = coupling.reshape(own_count, total_points, local_points, all_branches)
     rate_total = branch_total(jnp.sum(coupling, axis=(0, 1)))

time: 1070 us -> 914 us (0.85)
  blocking collectives: 635 us -> 448 us
  starting transfers between devices: 0 us -> 15.1 us
    all_gather x1 -> x0, blocking collectives: 164 us -> none  [on_device(): lax.all_gather(polarization, 'pb', axis=1, tiled=True)]
    psum x3, blocking collectives: 100 us -> 74.7 us  [branch_total(): summed = lax.psum(partial_sum, 'br')]
    all_to_all x0 -> x1, starting transfers between devices: none -> 15.1 us  [on_device(): lax.all_to_all(jnp.stack([polarization] * lax.axis_size('pb')), 'pb', 0, 0)]
  transfers between devices with their start and end apart: 0 -> 1, of which waited for: 0 -> 1; matrix products, arithmetic and copies ran while one was open for 0% -> 0% of each run, Pallas kernels for 0% -> 0%
where the time goes in v1:
time: 914 us; the launch traced here: 909 us
  blocking collectives  448 us (49%)
  local copies, waits for them, and re-layouts  237 us (26%)
  matrix products  99.9 us (11%)
  other arithmetic  96.8 us (11%)
  starting transfers between devices  15.1 us (2%)
  waiting for transfers between devices  10 us (1%)
    all_gather x2, blocking collectives, full_deviation(): return lax.all_gather(deviation, 'pb', axis=0, tiled=True)  299 us
    mul x8, local copies, waits for them, and re-layouts, per_point(): return jnp.sum(amplitude * amplitude, axis=2)  185 us
    reduce_sum x8, other arithmetic, per_point(): return jnp.sum(amplitude * amplitude, axis=2)  79.6 us
    dot_general x8, matrix products, per_point(): jnp.dot(flat_rows, const_block, preferred_element_type=jnp.float32)  77.6 us
    psum x3, blocking collectives, branch_total(): summed = lax.psum(partial_sum, 'br')  74.7 us
    psum x1, blocking collectives, on_device(): kappas.append(lax.psum(kappa_term, ('pb', 'br')))  74.3 us
    gather x2, local copies, waits for them, and re-layouts, on_device(): partner_value = deviation_all[partner]  28.1 us
    dot_general x2, matrix products, on_device(): jnp.einsum('abqs,abq->qs', coupling, combined, precision=lax.Precision.HI...  22.3 us
  transfers between devices with their start and end apart: 1, of which 1 were waited for; matrix products, arithmetic and copies ran while one was open for 0% of the time, Pallas kernels for 0%

profile of v1, /device:TPU:1, one launch (start us, length us, event | category | flops | bytes accessed | tf_op | source)
XLA Modules:
  0.0 908.6 jit_solution(9036719811943421128)
XLA Ops:
  1.5 2.5 reshape.47
  4.0 15.1 %all-to-all-start = ((bf16[64,2,1296]{2,1,0:T(2,128)(2,1)}), bf16[64,2,1296]{2,1,0:T(2,128)(2,1)S(1)}, u32[]{:S(2)}, u32[]{:S(2)}) async-start(bf16[64,2,1296]{2,1,0:T(2,128)(2,1)} %reshape.47), calls=%async_computation | async-start | bytes 720896 | tf_op jit(solution)/shard_map/all_to_all | solution.py:57
  19.1 2.4 reshape_reshape.6
  22.2 10.0 %all-to-all-done = bf16[64,2,1296]{2,1,0:T(2,128)(2,1)S(1)} async-done(((bf16[64,2,1296]{2,1,0:T(2,128)(2,1)}), bf16[64,2,1296]{2,1,0:T(2,128)(2,1)S(1)}, u32[]{:S(2)}, u32[]{:S(2)}) %all-to-all-start) | async-done | bytes 331808 | tf_op jit(solution)/shard_map/all_to_all | solution.py:57
  32.2 1.2 reshape.48
  33.6 350.0 %while.10 = (s32[]{:T(128)}, f32[8,4608,36]{1,2,0:T(8,128)}, bf16[8,36,1296]{2,1,0:T(8,128)(2,1)S(1)}, bf16[4608,36]{1,0:T(8,128)(2,1)S(1)}, s32[]{:T(128)}, /*index=5*/f32[]{:T(128)}) while((s32[]{:T(128)}, f32[8,4608,36]{1,2,0:T(8,128)}, bf16[8,36,1296]{2,1,0:T(8,128)(2,1)S(1)}, bf16[4608,36]{1,0:T(8,128)(2,1)S(1)}, s32[]{:T(128)}, ...), condition=%wide.region_2.3_spmd, body=%wide.region_0.2_spmd.sunk | while | flops 441759744 | bytes 98908744 | solution.py:27
  33.6 9.7 %fusion.18 = f32[4608,1296]{0,1:T(8,128)} fusion(bf16[4608,36]{1,0:T(8,128)(2,1)S(1)} %get-tuple-element.92, bf16[8,36,1296]{2,1,0:T(8,128)(2,1)S(1)} %get-tuple-element.91, s32[]{:T(128)} %get-tuple-element.83), kind=kOutput, calls=%fused_computation.3.clone.1 | convolution fusion | flops 435953664 | bytes 25180164 | tf_op jit(solution)/shard_map/while/body/eval_jaxpr/dot_general | solution.py:23
  43.4 23.2 %mul.74 = f32[4608,36,36]{0,2,1:T(8,128)} reshape(f32[4608,1296]{0,1:T(8,128)} %fusion.18) | data formatting | bytes 47775744 | tf_op jit(solution)/shard_map/while/body/eval_jaxpr/mul | solution.py:25
  66.5 9.9 %reduce_sum.46 = f32[4608,36]{0,1:T(8,128)S(1)} reduce(f32[4608,36,36]{0,2,1:T(8,128)} %mul.74, f32[]{:T(128)} %constant.7.clone.1..sunk), dimensions={2}, to_apply=%region_1.1 | reduce | flops 5806080 | bytes 24551428 | tf_op jit(solution)/shard_map/while/body/eval_jaxpr/reduce_sum | solution.py:25
  77.4 9.7 %fusion.18 = f32[4608,1296]{0,1:T(8,128)} fusion(bf16[4608,36]{1,0:T(8,128)(2,1)S(1)} %get-tuple-element.92, bf16[8,36,1296]{2,1,0:T(8,128)(2,1)S(1)} %get-tuple-element.91, s32[]{:T(128)} %get-tuple-element.83), kind=kOutput, calls=%fused_computation.3.clone.1 | convolution fusion | flops 435953664 | bytes 25180164 | tf_op jit(solution)/shard_map/while/body/eval_jaxpr/dot_general | solution.py:23
  87.1 23.2 %mul.74 = f32[4608,36,36]{0,2,1:T(8,128)} reshape(f32[4608,1296]{0,1:T(8,128)} %fusion.18) | data formatting | bytes 47775744 | tf_op jit(solution)/shard_map/while/body/eval_jaxpr/mul | solution.py:25
  110.2 9.9 %reduce_sum.46 = f32[4608,36]{0,1:T(8,128)S(1)} reduce(f32[4608,36,36]{0,2,1:T(8,128)} %mul.74, f32[]{:T(128)} %constant.7.clone.1..sunk), dimensions={2}, to_apply=%region_1.1 | reduce | flops 5806080 | bytes 24551428 | tf_op jit(solution)/shard_map/while/body/eval_jaxpr/reduce_sum | solution.py:25
  121.1 9.7 %fusion.18 = f32[4608,1296]{0,1:T(8,128)} fusion(bf16[4608,36]{1,0:T(8,128)(2,1)S(1)} %get-tuple-element.92, bf16[8,36,1296]{2,1,0:T(8,128)(2,1)S(1)} %get-tuple-element.91, s32[]{:T(128)} %get-tuple-element.83), kind=kOutput, calls=%fused_computation.3.clone.1 | convolution fusion | flops 435953664 | bytes 25180164 | tf_op jit(solution)/shard_map/while/body/eval_jaxpr/dot_general | solution.py:23
  130.8 23.2 %mul.74 = f32[4608,36,36]{0,2,1:T(8,128)} reshape(f32[4608,1296]{0,1:T(8,128)} %fusion.18) | data formatting | bytes 47775744 | tf_op jit(solution)/shard_map/while/body/eval_jaxpr/mul | solution.py:25
  154.0 9.9 %reduce_sum.46 = f32[4608,36]{0,1:T(8,128)S(1)} reduce(f32[4608,36,36]{0,2,1:T(8,128)} %mul.74, f32[]{:T(128)} %constant.7.clone.1..sunk), dimensions={2}, to_apply=%region_1.1 | reduce | flops 5806080 | bytes 24551428 | tf_op jit(solution)/shard_map/while/body/eval_jaxpr/reduce_sum | solution.py:25
  163.9 0.9 bitcast_dynamic-update-slice_fusion.2
  164.9 9.7 %fusion.18 = f32[4608,1296]{0,1:T(8,128)} fusion(bf16[4608,36]{1,0:T(8,128)(2,1)S(1)} %get-tuple-element.92, bf16[8,36,1296]{2,1,0:T(8,128)(2,1)S(1)} %get-tuple-element.91, s32[]{:T(128)} %get-tuple-element.83), kind=kOutput, calls=%fused_computation.3.clone.1 | convolution fusion | flops 435953664 | bytes 25180164 | tf_op jit(solution)/shard_map/while/body/eval_jaxpr/dot_general | solution.py:23
  174.6 23.2 %mul.74 = f32[4608,36,36]{0,2,1:T(8,128)} reshape(f32[4608,1296]{0,1:T(8,128)} %fusion.18) | data formatting | bytes 47775744 | tf_op jit(solution)/shard_map/while/body/eval_jaxpr/mul | solution.py:25
  197.7 9.9 %reduce_sum.46 = f32[4608,36]{0,1:T(8,128)S(1)} reduce(f32[4608,36,36]{0,2,1:T(8,128)} %mul.74, f32[]{:T(128)} %constant.7.clone.1..sunk), dimensions={2}, to_apply=%region_1.1 | reduce | flops 5806080 | bytes 24551428 | tf_op jit(solution)/shard_map/while/body/eval_jaxpr/reduce_sum | solution.py:25
  208.6 9.7 %fusion.18 = f32[4608,1296]{0,1:T(8,128)} fusion(bf16[4608,36]{1,0:T(8,128)(2,1)S(1)} %get-tuple-element.92, bf16[8,36,1296]{2,1,0:T(8,128)(2,1)S(1)} %get-tuple-element.91, s32[]{:T(128)} %get-tuple-element.83), kind=kOutput, calls=%fused_computation.3.clone.1 | convolution fusion | flops 435953664 | bytes 25180164 | tf_op jit(solution)/shard_map/while/body/eval_jaxpr/dot_general | solution.py:23
  218.3 23.2 %mul.74 = f32[4608,36,36]{0,2,1:T(8,128)} reshape(f32[4608,1296]{0,1:T(8,128)} %fusion.18) | data formatting | bytes 47775744 | tf_op jit(solution)/shard_map/while/body/eval_jaxpr/mul | solution.py:25
  241.5 9.9 %reduce_sum.46 = f32[4608,36]{0,1:T(8,128)S(1)} reduce(f32[4608,36,36]{0,2,1:T(8,128)} %mul.74, f32[]{:T(128)} %constant.7.clone.1..sunk), dimensions={2}, to_apply=%region_1.1 | reduce | flops 5806080 | bytes 24551428 | tf_op jit(solution)/shard_map/while/body/eval_jaxpr/reduce_sum | solution.py:25
  252.3 9.7 %fusion.18 = f32[4608,1296]{0,1:T(8,128)} fusion(bf16[4608,36]{1,0:T(8,128)(2,1)S(1)} %get-tuple-element.92, bf16[8,36,1296]{2,1,0:T(8,128)(2,1)S(1)} %get-tuple-element.91, s32[]{:T(128)} %get-tuple-element.83), kind=kOutput, calls=%fused_computation.3.clone.1 | convolution fusion | flops 435953664 | bytes 25180164 | tf_op jit(solution)/shard_map/while/body/eval_jaxpr/dot_general | solution.py:23
  262.1 23.2 %mul.74 = f32[4608,36,36]{0,2,1:T(8,128)} reshape(f32[4608,1296]{0,1:T(8,128)} %fusion.18) | data formatting | bytes 47775744 | tf_op jit(solution)/shard_map/while/body/eval_jaxpr/mul | solution.py:25
  285.2 9.9 %reduce_sum.46 = f32[4608,36]{0,1:T(8,128)S(1)} reduce(f32[4608,36,36]{0,2,1:T(8,128)} %mul.74, f32[]{:T(128)} %constant.7.clone.1..sunk), dimensions={2}, to_apply=%region_1.1 | reduce | flops 5806080 | bytes 24551428 | tf_op jit(solution)/shard_map/while/body/eval_jaxpr/reduce_sum | solution.py:25
  295.2 0.9 bitcast_dynamic-update-slice_fusion.2
  296.1 9.7 %fusion.18 = f32[4608,1296]{0,1:T(8,128)} fusion(bf16[4608,36]{1,0:T(8,128)(2,1)S(1)} %get-tuple-element.92, bf16[8,36,1296]{2,1,0:T(8,128)(2,1)S(1)} %get-tuple-element.91, s32[]{:T(128)} %get-tuple-element.83), kind=kOutput, calls=%fused_computation.3.clone.1 | convolution fusion | flops 435953664 | bytes 25180164 | tf_op jit(solution)/shard_map/while/body/eval_jaxpr/dot_general | solution.py:23
  305.8 23.2 %mul.74 = f32[4608,36,36]{0,2,1:T(8,128)} reshape(f32[4608,1296]{0,1:T(8,128)} %fusion.18) | data formatting | bytes 47775744 | tf_op jit(solution)/shard_map/while/body/eval_jaxpr/mul | solution.py:25
  329.0 9.9 %reduce_sum.46 = f32[4608,36]{0,1:T(8,128)S(1)} reduce(f32[4608,36,36]{0,2,1:T(8,128)} %mul.74, f32[]{:T(128)} %constant.7.clone.1..sunk), dimensions={2}, to_apply=%region_1.1 | reduce | flops 5806080 | bytes 24551428 | tf_op jit(solution)/shard_map/while/body/eval_jaxpr/reduce_sum | solution.py:25
  339.8 9.7 %fusion.18 = f32[4608,1296]{0,1:T(8,128)} fusion(bf16[4608,36]{1,0:T(8,128)(2,1)S(1)} %get-tuple-element.92, bf16[8,36,1296]{2,1,0:T(8,128)(2,1)S(1)} %get-tuple-element.91, s32[]{:T(128)} %get-tuple-element.83), kind=kOutput, calls=%fused_computation.3.clone.1 | convolution fusion | flops 435953664 | bytes 25180164 | tf_op jit(solution)/shard_map/while/body/eval_jaxpr/dot_general | solution.py:23
  349.5 23.2 %mul.74 = f32[4608,36,36]{0,2,1:T(8,128)} reshape(f32[4608,1296]{0,1:T(8,128)} %fusion.18) | data formatting | bytes 47775744 | tf_op jit(solution)/shard_map/while/body/eval_jaxpr/mul | solution.py:25
  372.7 9.9 %reduce_sum.46 = f32[4608,36]{0,1:T(8,128)S(1)} reduce(f32[4608,36,36]{0,2,1:T(8,128)} %mul.74, f32[]{:T(128)} %constant.7.clone.1..sunk), dimensions={2}, to_apply=%region_1.1 | reduce | flops 5806080 | bytes 24551428 | tf_op jit(solution)/shard_map/while/body/eval_jaxpr/reduce_sum | solution.py:25
  383.6 7.2 reshape.21
  390.8 9.9 %fusion.9 = (f32[288]{0:T(512)S(1)}, f32[9,512,288]{1,0,2:T(8,128)}) fusion(f32[9,512,288]{1,0,2:T(8,128)} %reshape.21, bf16[9,512,288]{1,2,0:T(8,128)(2,1)S(1)} %copy-done), kind=kLoop, calls=%fused_computation.24 | loop fusion | flops 5308128 | bytes 13272192 | tf_op jit(solution)/shard_map/reduce_sum | solution.py:62
  400.8 8.2 psum.35
  409.1 151.1 %all_gather.6 = f32[512,9]{1,0:T(8,128)S(1)} all-gather(f32[8,9]{1,0:T(8,128)S(1)} %dynamic-slice_divide_fusion), channel_id=1, replica_groups=mesh['pb'=64,'br'=4] {'pb'}, dimensions={0}, use_global_device_ids=true | all-gather | bytes 18720 | tf_op jit(solution)/shard_map/all_gather | solution.py:40
  560.2 14.1 %gather_fusion = f32[4096,9]{1,0:T(8,128)} fusion(f32[512,9]{1,0:T(8,128)S(1)} %all_gather.6, s32[4096]{0:T(1024)S(1)} %copy-done.1), kind=kCustom, calls=%fused_computation | custom fusion | bytes 311296 | tf_op jit(solution)/shard_map/gather | solution.py:68
  574.2 1.7 add_bitcast_fusion.1
  576.8 11.1 %fusion.6 = f32[8,1,36,1]{2,1,0,3:T(1,128)S(1)} fusion(f32[9,512,8,1]{1,3,2,0:T(1,128)S(1)} %copy.19, f32[9,512,8,36]{1,0,3,2:T(8,128)} %bitcast.52), kind=kOutput, calls=%fused_computation.11 | convolution fusion | flops 15925248 | bytes 5457024 | tf_op jit(solution)/shard_map/abqs,abq->qs/dot_general | solution.py:72
  588.0 33.3 %psum.36 = f32[8,36]{1,0:T(8,128)S(1)} all-reduce(f32[8,36]{1,0:T(8,128)S(1)} %bitcast.62), channel_id=1, replica_groups=mesh['pb'=64,'br'=4] {'br'}, use_global_device_ids=true, to_apply=%region_5.6 | all-reduce | flops 288 | bytes 2304 | tf_op jit(solution)/shard_map/psum | solution.py:35
  621.4 147.7 %all_gather.7 = f32[512,9]{1,0:T(8,128)S(1)} all-gather(f32[8,9]{1,0:T(8,128)S(1)} %add_divide_fusion.1), channel_id=1, replica_groups=mesh['pb'=64,'br'=4] {'pb'}, dimensions={0}, use_global_device_ids=true | all-gather | bytes 18720 | tf_op jit(solution)/shard_map/all_gather | solution.py:40
  769.1 14.1 %gather_fusion.1 = f32[4096,9]{1,0:T(8,128)} fusion(f32[512,9]{1,0:T(8,128)S(1)} %all_gather.7, s32[4096]{0:T(1024)S(1)} %copy-done.1), kind=kCustom, calls=%fused_computation.1 | custom fusion | bytes 311296 | tf_op jit(solution)/shard_map/gather | solution.py:68
  783.1 1.8 add_bitcast_fusion
  785.7 11.1 %fusion.4 = f32[8,1,36,1]{2,1,0,3:T(1,128)S(1)} fusion(f32[9,512,8,1]{1,3,2,0:T(1,128)S(1)} %copy.21, f32[9,512,8,36]{1,0,3,2:T(8,128)} %bitcast.53), kind=kOutput, calls=%fused_computation.9 | convolution fusion | flops 15925248 | bytes 5457024 | tf_op jit(solution)/shard_map/abqs,abq->qs/dot_general | solution.py:72
  796.9 33.2 %psum.37 = f32[8,36]{1,0:T(8,128)S(1)} all-reduce(f32[8,36]{1,0:T(8,128)S(1)} %bitcast.61), channel_id=1, replica_groups=mesh['pb'=64,'br'=4] {'br'}, use_global_device_ids=true, to_apply=%region_6.7 | all-reduce | flops 288 | bytes 2304 | tf_op jit(solution)/shard_map/psum | solution.py:35
  830.1 1.3 multiply_reduce_fusion.1
  832.5 74.3 %all-reduce = (f32[1]{0:T(128)}, f32[1]{0:T(128)}) all-reduce(f32[1]{0:T(128)} %bitcast.21, f32[1]{0:T(128)} %bitcast.20), channel_id=1, replica_groups=mesh['pb'=64,'br'=4] {'pb','br'}, use_global_device_ids=true, to_apply=%region_10.11 | all-reduce | flops 2 | bytes 16 | tf_op jit(solution)/shard_map/psum | solution.py:76
  906.9 1.8 pad_maximum_fusion
  (28 shorter events, 9.3 us)
Async XLA Ops:
  0.6 20.9 %copy-start.3 = (s32[8,512]{1,0:T(8,128)S(1)}, s32[8,512]{1,0:T(8,128)}, u32[]{:S(2)}) copy-start(s32[8,512]{1,0:T(8,128)} %param.11) | copy-start | bytes 49156
  4.0 28.2 %all-to-all-start = ((bf16[64,2,1296]{2,1,0:T(2,128)(2,1)}), bf16[64,2,1296]{2,1,0:T(2,128)(2,1)S(1)}, u32[]{:S(2)}, u32[]{:S(2)}) async-start(bf16[64,2,1296]{2,1,0:T(2,128)(2,1)} %reshape.47), calls=%async_computation | async-start | bytes 720896 | tf_op jit(solution)/shard_map/all_to_all | solution.py:57
  383.6 7.2 copy-start
  390.8 18.2 %copy-start.2 = (f32[8,9]{1,0:T(8,128)S(1)}, f32[8,9]{1,0:T(8,128)}, u32[]{:S(2)}) copy-start(f32[8,9]{1,0:T(8,128)} %param.12) | copy-start | bytes 868
  390.8 169.4 %copy-start.1 = (s32[4096]{0:T(1024)S(1)}, s32[4096]{0:T(1024)}, u32[]{:S(2)}) copy-start(s32[4096]{0:T(1024)} %broadcast_clamp_fusion) | copy-start | bytes 49156
  783.1 46.9 %copy-start.4 = (f32[8,9]{1,0:T(8,128)S(1)}, f32[8,9]{1,0:T(8,128)}, u32[]{:S(2)}) copy-start(f32[8,9]{1,0:T(8,128)} %param.13) | copy-start | bytes 868
